TPU v7x, 32 devices: a whole 2x2x4 slice. The times are simulated.
32 devices in a mesh: dp: 1, ctx: 32 (over z, y, x, core).
Axes of the slice: x: 2, y: 2, z: 4, core: 2. Of those that a mesh axis runs over, the one named last changes fastest.
Arguments:
- queries: bfloat16 [4096, 8192], P(('dp', 'ctx')), may hold values from -16 to 16
- out_grad: bfloat16 [4096, 8192], P(('dp', 'ctx')), may hold values from -6 to 6
- enc_states: bfloat16 [384, 1024], P(('dp', 'ctx')), may hold values from -8 to 8
- w_key: bfloat16 [1024, 8192], P('dp', 'ctx'), may hold values from -1 to 1
- w_value: bfloat16 [1024, 8192], P('dp', 'ctx'), may hold values from -0.1875 to 0.1875
- dec_segments: int32 [4096], P(('dp', 'ctx')), may hold values from 0 to 3, as said below
- enc_segments: int32 [384], P(('dp', 'ctx')), may hold values from 0 to 3, as said below
Outputs:
- query_grad: bfloat16 [4096, 8192], P(('dp', 'ctx'))
- enc_grad: bfloat16 [384, 1024], P(('dp', 'ctx'))
- w_key_grad: float32 [1024, 8192], P('dp', 'ctx')
- w_value_grad: float32 [1024, 8192], P('dp', 'ctx')
Inputs may be any that keep to these rules, and one draw needn't show every extreme that they name: `dec_segments`: within each pack the ids never fall along the tokens, and each of the 4 ids has one or more decoder tokens in the pack. `enc_segments`: within each pack the ids never fall along the tokens, and each of the 4 ids has two or more encoder tokens in the pack.
All inputs are finite; a program needn't handle non-finite values.
Results may differ from a plain program's by a relative error of at most 0.019.
Values may be sent and summed in bfloat16 or wider, within the bound.
A program may use at most 64 MiB of HBM per device.

v0:
```python
import math
import jax
import jax.numpy as jnp
from jax import lax
from jax.sharding import PartitionSpec as P

HEAD_DIM = 128


def attend(queries, out_grads, key_rows, value_rows, query_ids, key_ids):
    length, full_width = queries.shape
    key_count = key_rows.shape[0]
    head_count = full_width // HEAD_DIM
    group_size = min(head_count, 16)
    column_count = group_size * HEAD_DIM
    row_count = math.gcd(length, 1024)

    def head_group(number):
        column_start = number * column_count
        key_block = key_rows.reshape(key_count, group_size, HEAD_DIM)
        value_block = value_rows.reshape(key_count, group_size, HEAD_DIM)

        def query_block(totals, block_number):
            first_row = block_number * row_count
            query_part = lax.dynamic_slice(
                queries, (first_row, column_start), (row_count, column_count)
            ).reshape(row_count, group_size, HEAD_DIM)
            grad_part = lax.dynamic_slice(
                out_grads, (first_row, column_start), (row_count, column_count)
            ).reshape(row_count, group_size, HEAD_DIM)
            block_ids = lax.dynamic_slice_in_dim(query_ids, first_row, row_count, 0)
            allowed = block_ids[:, None] == key_ids[None, :]
            scores = jnp.einsum(
                "qhd,khd->hqk", query_part, key_block, preferred_element_type=jnp.float32
            )
            scores = jnp.where(allowed[None], scores, -jnp.inf)
            highest = jnp.max(scores, axis=2, keepdims=True)
            weights = jnp.exp(scores - highest)
            probability = weights / jnp.sum(weights, axis=2, keepdims=True)
            upstream = jnp.einsum(
                "qhd,khd->hqk", grad_part, value_block, preferred_element_type=jnp.float32
            )
            row_dot = jnp.sum(probability * upstream, axis=2, keepdims=True)
            score_grad = (probability * (upstream - row_dot)).astype(jnp.bfloat16)
            rounded = probability.astype(jnp.bfloat16)
            key_total = totals[0] + jnp.einsum(
                "hqk,qhd->khd", score_grad, query_part, preferred_element_type=jnp.float32
            )
            value_total = totals[1] + jnp.einsum(
                "hqk,qhd->khd", rounded, grad_part, preferred_element_type=jnp.float32
            )
            totals = (key_total, value_total)
            query_grad = jnp.einsum(
                "hqk,khd->qhd", score_grad, key_block, preferred_element_type=jnp.float32
            ).astype(jnp.bfloat16)
            return (totals, query_grad.reshape(row_count, column_count))

        zeros = jnp.zeros((key_count, group_size, HEAD_DIM), jnp.float32)
        totals, query_grads = lax.scan(
            query_block, (zeros, zeros), jnp.arange(length // row_count, dtype=jnp.int32)
        )
        results = ()
        results = results + (query_grads.reshape(length, column_count),)
        results = results + (
            totals[0].reshape(key_count, column_count),
            totals[1].reshape(key_count, column_count),
        )
        return results

    pieces = lax.map(head_group, jnp.arange(head_count // group_size, dtype=jnp.int32))
    return tuple(
        (jnp.moveaxis(piece, 0, 1).reshape(piece.shape[1], full_width) for piece in pieces)
    )


def body(queries, out_grad, enc_states, w_key, w_value, dec_segments, enc_segments):
    encoder, key_ids = (
        lax.all_gather(enc_states, "ctx", axis=0, tiled=True),
        lax.all_gather(enc_segments, "ctx", axis=0, tiled=True),
    )
    key_weight, value_weight = (
        lax.all_gather(w_key, "dp", axis=0, tiled=True),
        lax.all_gather(w_value, "dp", axis=0, tiled=True),
    )
    key_part = jnp.dot(encoder, key_weight, preferred_element_type=jnp.float32).astype(jnp.bfloat16)
    value_part = jnp.dot(encoder, value_weight, preferred_element_type=jnp.float32).astype(
        jnp.bfloat16
    )
    local_queries, local_grads = (
        lax.all_to_all(queries, "ctx", split_axis=1, concat_axis=0, tiled=True),
        lax.all_to_all(out_grad, "ctx", split_axis=1, concat_axis=0, tiled=True),
    )
    query_ids = lax.all_gather(dec_segments, "ctx", axis=0, tiled=True)
    head_grad, key_grad, value_grad = attend(
        local_queries, local_grads, key_part, value_part, query_ids, key_ids
    )
    query_grad = lax.all_to_all(head_grad, "ctx", split_axis=0, concat_axis=1, tiled=True)
    key_round = key_grad.astype(jnp.bfloat16)
    value_round = value_grad.astype(jnp.bfloat16)
    across = (((1,), (1,)), ((), ()))
    partial_value = lax.dot_general(
        key_round, key_weight, across, preferred_element_type=jnp.float32
    )
    partial_value = partial_value + lax.dot_general(
        value_round, value_weight, across, preferred_element_type=jnp.float32
    )
    enc_grad = lax.psum_scatter(
        partial_value.astype(jnp.bfloat16), "ctx", scatter_dimension=0, tiled=True
    )
    down = (((0,), (0,)), ((), ()))
    key_term = lax.dot_general(encoder, key_round, down, preferred_element_type=jnp.float32)
    value_term = lax.dot_general(encoder, value_round, down, preferred_element_type=jnp.float32)
    w_key_grad, w_value_grad = (
        lax.psum_scatter(
            key_term.astype(jnp.bfloat16), "dp", scatter_dimension=0, tiled=True
        ).astype(jnp.float32),
        lax.psum_scatter(
            value_term.astype(jnp.bfloat16), "dp", scatter_dimension=0, tiled=True
        ).astype(jnp.float32),
    )
    return (query_grad, enc_grad, w_key_grad, w_value_grad)


def solution(mesh):
    in_specs = (
        P(("dp", "ctx"), None),
        P(("dp", "ctx"), None),
        P(("dp", "ctx"), None),
        P("dp", "ctx"),
        P("dp", "ctx"),
        P(("dp", "ctx")),
        P(("dp", "ctx")),
    )
    out_specs = (P(("dp", "ctx"), None), P(("dp", "ctx"), None), P("dp", "ctx"), P("dp", "ctx"))
    return jax.shard_map(body, mesh=mesh, in_specs=in_specs, out_specs=out_specs, check_vma=False)
```

profile of v0, /device:TPU:3, one launch (start us, length us, event | category | flops | bytes accessed | tf_op | source)
XLA Modules:
  0.0 431.3 jit_solution(11465788982890251709)
XLA Ops:
  0.6 4.1 copy.68
  4.8 6.5 %all-to-all-start = ((bf16[128,32,256]{0,2,1:T(8,128)(2,1)}), bf16[128,32,256]{0,2,1:T(8,128)(2,1)}, u32[]{:S(2)}, u32[]{:S(2)}) async-start(bf16[128,32,256]{0,2,1:T(8,128)(2,1)} %bitcast.97), calls=%async_computation | async-start | bytes 4194304 | tf_op jit(solution)/shard_map/all_to_all | solution.py:90
  11.2 4.1 copy.70
  15.4 43.9 %all-to-all-done = bf16[128,32,256]{0,2,1:T(8,128)(2,1)} async-done(((bf16[128,32,256]{0,2,1:T(8,128)(2,1)}), bf16[128,32,256]{0,2,1:T(8,128)(2,1)}, u32[]{:S(2)}, u32[]{:S(2)}) %all-to-all-start) | async-done | bytes 2097184 | tf_op jit(solution)/shard_map/all_to_all | solution.py:90
  59.3 4.9 %all-to-all-start.1 = ((bf16[128,32,256]{0,2,1:T(8,128)(2,1)}), bf16[128,32,256]{0,2,1:T(8,128)(2,1)}, u32[]{:S(2)}, u32[]{:S(2)}) async-start(bf16[128,32,256]{0,2,1:T(8,128)(2,1)} %bitcast.96), calls=%async_computation.1 | async-start | bytes 4194304 | tf_op jit(solution)/shard_map/all_to_all | solution.py:91
  64.2 72.7 %all-gather.1 = bf16[32,12,1024]{2,1,0:T(8,128)(2,1)S(1)} all-gather(bf16[1,12,1024]{2,1,0:T(8,128)(2,1)S(1)} %bitcast.107), channel_id=1, replica_groups=mesh['dp'=1,'ctx'=32] {'ctx'}, dimensions={0}, use_global_device_ids=true | all-gather | bytes 811008 | tf_op jit(solution)/shard_map/all_gather | solution.py:78
  137.6 0.8 copy.74
  138.6 41.9 %all-reduce = s32[384]{0:T(512)S(1)} all-reduce(s32[384]{0:T(512)S(1)} %dynamic-update-slice), channel_id=1, replica_groups=mesh['dp'=1,'ctx'=32] {'ctx'}, use_global_device_ids=true, to_apply=%add | all-reduce | flops 384 | bytes 3072
  180.6 37.8 %all-gather = s32[32,1,128]{2,1,0:T(1,128)S(1)} all-gather(s32[1,1,128]{2,1,0:T(1,128)S(1)} %bitcast.108), channel_id=1, replica_groups=mesh['dp'=1,'ctx'=32] {'ctx'}, dimensions={0}, use_global_device_ids=true | all-gather | bytes 16896 | tf_op jit(solution)/shard_map/all_gather | solution.py:93
  218.8 4.1 copy.69
  222.9 4.1 copy.71
  227.0 57.9 %while.27 = (s32[]{:T(128)}, f32[384,2,128]{0,2,1:T(8,128)S(1)}, f32[384,2,128]{0,2,1:T(8,128)}, bf16[4,1024,256]{2,1,0:T(8,128)(2,1)}, s32[4]{0:T(128)S(1)}, /*...) while((s32[]{:T(128)}, f32[384,2,128]{0,2,1:T(8,128)S(1)}, ...), condition=%wide.region_4.5_spmd.clone, body=%wide.region_0.4_spmd.clone.sunk | while | flops 1017117056 | bytes 52033364 | solution.py:59
  228.3 1.0 broadcast_compare_fusion.2
  229.3 1.3 constant_dynamic-slice_fusion.4
  231.0 4.0 fusion.71
  235.0 2.7 fusion.73
  240.7 0.8 constant_dynamic-update-slice_fusion.2
  242.7 1.0 broadcast_compare_fusion.2
  243.8 1.3 constant_dynamic-slice_fusion.4
  245.5 3.9 fusion.71
  249.4 2.7 fusion.73
  255.1 0.8 constant_dynamic-update-slice_fusion.2
  257.2 1.0 broadcast_compare_fusion.2
  258.3 1.3 constant_dynamic-slice_fusion.4
  260.0 4.0 fusion.71
  263.9 2.7 fusion.73
  269.6 0.8 constant_dynamic-update-slice_fusion.2
  271.7 1.0 broadcast_compare_fusion.2
  272.7 1.3 constant_dynamic-slice_fusion.4
  274.4 4.0 fusion.71
  278.4 2.7 fusion.73
  284.1 0.8 constant_dynamic-update-slice_fusion.2
  284.9 7.4 %all-to-all-start.2 = ((bf16[32,128,256]{2,1,0:T(8,128)(2,1)}), bf16[32,128,256]{2,1,0:T(8,128)(2,1)}, u32[]{:S(2)}, u32[]{:S(2)}) async-start(bf16[32,128,256]{2,1,0:T(8,128)(2,1)} %bitcast.100), calls=%async_computation.2 | async-start | bytes 4194304 | tf_op jit(solution)/shard_map/all_to_all | solution.py:97
  293.8 94.7 %fusion = bf16[16,1024]{1,0:T(8,128)(2,1)S(1)} fusion(bf16[384,1024]{1,0:T(8,128)(2,1)S(1)} %add_convert_fusion), kind=kCustom, calls=%all-reduce-scatter | all-reduce-scatter fusion | flops 524289 | bytes 819200
  388.5 1.3 collective-permute-start.6
  389.8 8.5 %collective-permute-start.5 = (bf16[16,1024]{1,0:T(8,128)(2,1)S(1)}, bf16[16,1024]{1,0:T(8,128)(2,1)S(1)}, u32[]{:S(2)}, u32[]{:S(2)}) collective-permute-start(bf16[16,1024]{1,0:T(8,128)(2,1)S(1)} %fusion), channel_id=1, source_target_pairs={{0,6},{1,7},{2,8},{3,9},{4,10},{5,11},{6,12},{7,13},{8,14},{9,15},... | collective-permute-start | bytes 98312
  398.3 1.3 collective-permute-start.7
  400.1 2.8 collective-permute-start.4
  402.9 1.3 collective-permute-start.3
  404.2 5.9 %collective-permute-start.2 = (bf16[16,1024]{1,0:T(8,128)(2,1)S(1)}, bf16[16,1024]{1,0:T(8,128)(2,1)S(1)}, u32[]{:S(2)}, u32[]{:S(2)}) collective-permute-start(bf16[16,1024]{1,0:T(8,128)(2,1)S(1)} %fusion), channel_id=1, source_target_pairs={{0,3},{1,4},{2,5},{3,6},{4,7},{5,8},{6,9},{7,10},{8,11},{9,12},{10... | collective-permute-start | bytes 98312
  410.2 2.5 collective-permute-start.1
  412.7 4.5 %collective-permute-start = (bf16[16,1024]{1,0:T(8,128)(2,1)S(1)}, bf16[16,1024]{1,0:T(8,128)(2,1)S(1)}, u32[]{:S(2)}, u32[]{:S(2)}) collective-permute-start(bf16[16,1024]{1,0:T(8,128)(2,1)S(1)} %fusion), channel_id=1, source_target_pairs={{0,1},{1,2},{2,3},{3,4},{4,5},{5,6},{6,7},{7,8},{8,9},{9,10},{10,1... | collective-permute-start | bytes 98312
  417.3 1.4 fusion.20
  418.7 1.3 copy.79
  420.0 1.3 copy.78
  421.4 1.2 concatenate
  423.2 4.1 copy.76
  427.2 4.1 copy.77
  (110 shorter events, 19.6 us)
Async XLA Ops:
  0.6 217.7 %copy-start = (bf16[1024,256]{1,0:T(8,128)(2,1)S(1)}, bf16[1024,256]{1,0:T(8,128)(2,1)}, u32[]{:S(2)}) copy-start(bf16[1024,256]{1,0:T(8,128)(2,1)} %param.12) | copy-start | bytes 1572868
  4.8 54.5 %all-to-all-start = ((bf16[128,32,256]{0,2,1:T(8,128)(2,1)}), bf16[128,32,256]{0,2,1:T(8,128)(2,1)}, u32[]{:S(2)}, u32[]{:S(2)}) async-start(bf16[128,32,256]{0,2,1:T(8,128)(2,1)} %bitcast.97), calls=%async_computation | async-start | bytes 4194304 | tf_op jit(solution)/shard_map/all_to_all | solution.py:90
  59.3 5.0 %copy-start.9 = (bf16[12,1024]{1,0:T(8,128)(2,1)S(1)}, bf16[12,1024]{1,0:T(8,128)(2,1)}, u32[]{:S(2)}) copy-start(bf16[12,1024]{1,0:T(8,128)(2,1)} %param.11) | copy-start | bytes 73732
  59.3 163.7 %all-to-all-start.1 = ((bf16[128,32,256]{0,2,1:T(8,128)(2,1)}), bf16[128,32,256]{0,2,1:T(8,128)(2,1)}, u32[]{:S(2)}, u32[]{:S(2)}) async-start(bf16[128,32,256]{0,2,1:T(8,128)(2,1)} %bitcast.96), calls=%async_computation.1 | async-start | bytes 4194304 | tf_op jit(solution)/shard_map/all_to_all | solution.py:91
  64.2 72.9 %copy-start.3 = (bf16[1024,256]{1,0:T(8,128)(2,1)S(1)}, bf16[1024,256]{1,0:T(8,128)(2,1)}, u32[]{:S(2)}) copy-start(bf16[1024,256]{1,0:T(8,128)(2,1)} %param.13) | copy-start | bytes 1572868
  136.9 1.5 copy-start.11
  136.9 43.6 %copy-start.10 = (s32[128]{0:T(128)S(1)}, s32[128]{0:T(128)}, u32[]{:S(2)}) copy-start(s32[128]{0:T(128)} %param.14) | copy-start | bytes 1540
  231.0 4.0 copy-start.5
  235.0 2.8 copy-start.1
  235.0 2.8 copy-start.8
  237.8 0.7 copy-start.6
  245.5 4.0 copy-start.5
  249.4 2.8 copy-start.1
  249.4 2.8 copy-start.8
  252.3 0.7 copy-start.6
  260.0 4.0 copy-start.5
  263.9 2.8 copy-start.1
  263.9 2.8 copy-start.8
  266.8 0.7 copy-start.6
  274.4 4.0 copy-start.5
  278.4 2.8 copy-start.1
  278.4 2.8 copy-start.8
  281.2 0.7 copy-start.6
  284.9 7.5 %copy-start.7 = (f32[384,2,128]{0,2,1:T(8,128)S(1)}, f32[384,2,128]{0,2,1:T(8,128)}, u32[]{:S(2)}) copy-start(f32[384,2,128]{0,2,1:T(8,128)} %get-tuple-element.121) | copy-start | bytes 1179652
  284.9 138.3 %all-to-all-start.2 = ((bf16[32,128,256]{2,1,0:T(8,128)(2,1)}), bf16[32,128,256]{2,1,0:T(8,128)(2,1)}, u32[]{:S(2)}, u32[]{:S(2)}) async-start(bf16[32,128,256]{2,1,0:T(8,128)(2,1)} %bitcast.100), calls=%async_computation.2 | async-start | bytes 4194304 | tf_op jit(solution)/shard_map/all_to_all | solution.py:97
  292.3 1.0 copy-start.4
  388.5 21.6 %collective-permute-start.6 = (bf16[16,1024]{1,0:T(8,128)(2,1)S(1)}, bf16[16,1024]{1,0:T(8,128)(2,1)S(1)}, u32[]{:S(2)}, u32[]{:S(2)}) collective-permute-start(bf16[16,1024]{1,0:T(8,128)(2,1)S(1)} %fusion), channel_id=1, source_target_pairs={{0,7},{1,8},{2,9},{3,10},{4,11},{5,12},{6,13},{7,14},{8,15},{9,16}... | collective-permute-start | bytes 98312
  389.8 22.9 %collective-permute-start.5 = (bf16[16,1024]{1,0:T(8,128)(2,1)S(1)}, bf16[16,1024]{1,0:T(8,128)(2,1)S(1)}, u32[]{:S(2)}, u32[]{:S(2)}) collective-permute-start(bf16[16,1024]{1,0:T(8,128)(2,1)S(1)} %fusion), channel_id=1, source_target_pairs={{0,6},{1,7},{2,8},{3,9},{4,10},{5,11},{6,12},{7,13},{8,14},{9,15},... | collective-permute-start | bytes 98312
  398.3 5.9 %collective-permute-start.7 = (bf16[12,1024]{1,0:T(8,128)(2,1)S(1)}, bf16[12,1024]{1,0:T(8,128)(2,1)S(1)}, u32[]{:S(2)}, u32[]{:S(2)}) collective-permute-start(bf16[12,1024]{1,0:T(8,128)(2,1)S(1)} %slice), channel_id=1, source_target_pairs={{0,8},{1,9},{2,10},{3,11},{4,12},{5,13},{6,14},{7,15},{8,16},{9,17... | collective-permute-start | bytes 73736
  400.1 21.3 %collective-permute-start.4 = (bf16[16,1024]{1,0:T(8,128)(2,1)S(1)}, bf16[16,1024]{1,0:T(8,128)(2,1)S(1)}, u32[]{:S(2)}, u32[]{:S(2)}) collective-permute-start(bf16[16,1024]{1,0:T(8,128)(2,1)S(1)} %fusion), channel_id=1, source_target_pairs={{0,5},{1,6},{2,7},{3,8},{4,9},{5,10},{6,11},{7,12},{8,13},{9,14},{... | collective-permute-start | bytes 98312
  402.9 18.4 %collective-permute-start.3 = (bf16[16,1024]{1,0:T(8,128)(2,1)S(1)}, bf16[16,1024]{1,0:T(8,128)(2,1)S(1)}, u32[]{:S(2)}, u32[]{:S(2)}) collective-permute-start(bf16[16,1024]{1,0:T(8,128)(2,1)S(1)} %fusion), channel_id=1, source_target_pairs={{0,4},{1,5},{2,6},{3,7},{4,8},{5,9},{6,10},{7,11},{8,12},{9,13},{1... | collective-permute-start | bytes 98312
  404.2 17.1 %collective-permute-start.2 = (bf16[16,1024]{1,0:T(8,128)(2,1)S(1)}, bf16[16,1024]{1,0:T(8,128)(2,1)S(1)}, u32[]{:S(2)}, u32[]{:S(2)}) collective-permute-start(bf16[16,1024]{1,0:T(8,128)(2,1)S(1)} %fusion), channel_id=1, source_target_pairs={{0,3},{1,4},{2,5},{3,6},{4,7},{5,8},{6,9},{7,10},{8,11},{9,12},{10... | collective-permute-start | bytes 98312
  410.2 11.2 %collective-permute-start.1 = (bf16[16,1024]{1,0:T(8,128)(2,1)S(1)}, bf16[16,1024]{1,0:T(8,128)(2,1)S(1)}, u32[]{:S(2)}, u32[]{:S(2)}) collective-permute-start(bf16[16,1024]{1,0:T(8,128)(2,1)S(1)} %fusion), channel_id=1, source_target_pairs={{0,2},{1,3},{2,4},{3,5},{4,6},{5,7},{6,8},{7,9},{8,10},{9,11},{10,... | collective-permute-start | bytes 98312
  412.7 8.6 %collective-permute-start = (bf16[16,1024]{1,0:T(8,128)(2,1)S(1)}, bf16[16,1024]{1,0:T(8,128)(2,1)S(1)}, u32[]{:S(2)}, u32[]{:S(2)}) collective-permute-start(bf16[16,1024]{1,0:T(8,128)(2,1)S(1)} %fusion), channel_id=1, source_target_pairs={{0,1},{1,2},{2,3},{3,4},{4,5},{5,6},{6,7},{7,8},{8,9},{9,10},{10,1... | collective-permute-start | bytes 98312
  418.7 1.3 copy-start.2
where the time goes:
time: 433 us; the launch traced here: 431 us
  blocking collectives  247 us (57%)
  starting transfers between devices  47 us (11%)
  local copies, waits for them, and re-layouts  45 us (10%)
  waiting for transfers between devices  43.9 us (10%)
  matrix products  37 us (9%)
  other arithmetic  7.34 us (2%)
    unnamed x2, blocking collectives  137 us
    all_gather x1, blocking collectives, body(): lax.all_gather(enc_states, 'ctx', axis=0, tiled=True)  72.7 us
    all_to_all x1, waiting for transfers between devices, body(): lax.all_to_all(queries, 'ctx', split_axis=1, concat_axis=0, tiled=True)  43.9 us
    all_gather x1, blocking collectives, body(): query_ids = lax.all_gather(dec_segments, 'ctx', axis=0, tiled=True)  37.8 us
    unnamed x8, starting transfers between devices  28.2 us
    unnamed x28, local copies, waits for them, and re-layouts  18.5 us
    sub x4, matrix products, query_block(): weights = jnp.exp(scores - highest)  15.8 us
    dot_general x4, matrix products, query_block(): jnp.einsum('hqk,qhd->khd', rounded, grad_part, preferred_element_type=jnp...  10.9 us
  transfers between devices with their start and end apart: 11, of which 1 were waited for; matrix products, arithmetic and copies ran while one was open for 26% of the time, Pallas kernels for 0%

commit v1 on v0

--- a/solution.py
+++ b/solution.py
@@ -87,7 +87,12 @@
         jnp.bfloat16
     )
     local_queries, local_grads = (
-        lax.all_to_all(queries, "ctx", split_axis=1, concat_axis=0, tiled=True),
+        jnp.concatenate(
+            lax.all_to_all(
+                jnp.stack(jnp.split(queries, lax.axis_size("ctx"), axis=1)), "ctx", 0, 0
+            ),
+            axis=0,
+        ),
         lax.all_to_all(out_grad, "ctx", split_axis=1, concat_axis=0, tiled=True),
     )
     query_ids = lax.all_gather(dec_segments, "ctx", axis=0, tiled=True)

time: 433 us -> 432 us (level)
  waiting for transfers between devices: 43.9 us -> 1.19 us
  local copies, waits for them, and re-layouts: 45 us -> 85.2 us
    all_to_all x1, waiting for transfers between devices: 43.9 us -> 0.01 us  [body(): lax.all_to_all(jnp.stack(jnp.split(queries, lax.axis_size('ctx'), axis=1)...]
    unnamed x28 -> x62, local copies, waits for them, and re-layouts: 18.5 us -> 62.1 us
  transfers between devices with their start and end apart: 11 -> 11, of which waited for: 1 -> 1; matrix products, arithmetic and copies ran while one was open for 26% -> 37% of each run, Pallas kernels for 0% -> 0%
where the time goes in v1:
time: 432 us; the launch traced here: 428 us
  blocking collectives  247 us (57%)
  local copies, waits for them, and re-layouts  85.2 us (20%)
  starting transfers between devices  47.1 us (11%)
  matrix products  36.1 us (8%)
  other arithmetic  7.34 us (2%)
    unnamed x2, blocking collectives  137 us
    all_gather x1, blocking collectives, body(): lax.all_gather(enc_states, 'ctx', axis=0, tiled=True)  72.7 us
    unnamed x62, local copies, waits for them, and re-layouts  62.1 us
    all_gather x1, blocking collectives, body(): query_ids = lax.all_gather(dec_segments, 'ctx', axis=0, tiled=True)  37.8 us
    unnamed x8, starting transfers between devices  28.4 us
    sub x4, matrix products, query_block(): weights = jnp.exp(scores - highest)  15.8 us
    dot_general x4, matrix products, query_block(): jnp.einsum('hqk,qhd->khd', rounded, grad_part, preferred_element_type=jnp...  10.9 us
  transfers between devices with their start and end apart: 11, of which 1 were waited for; matrix products, arithmetic and copies ran while one was open for 37% of the time, Pallas kernels for 0%

profile of v1, /device:TPU:3, one launch (start us, length us, event | category | flops | bytes accessed | tf_op | source)
XLA Modules:
  0.0 427.8 jit_solution(15906440587263924205)
XLA Ops:
  0.6 4.1 copy.68
  4.8 6.4 %all-to-all-start.1 = ((bf16[128,32,256]{0,2,1:T(8,128)(2,1)}), bf16[128,32,256]{0,2,1:T(8,128)(2,1)S(1)}, u32[]{:S(2)}, u32[]{:S(2)}) async-start(bf16[128,32,256]{0,2,1:T(8,128)(2,1)} %bitcast.156), calls=%async_computation.1 | async-start | bytes 4194304 | tf_op jit(solution)/shard_map/all_to_all | solution.py:96
  11.2 1.5 constant_dynamic-update-slice_fusion.32
  12.7 1.5 constant_dynamic-update-slice_fusion.31
  17.0 1.5 constant_dynamic-update-slice_fusion.28
  21.4 1.5 constant_dynamic-update-slice_fusion.25
  24.3 1.5 constant_dynamic-update-slice_fusion.23
  25.8 1.5 constant_dynamic-update-slice_fusion.22
  27.3 1.5 constant_dynamic-update-slice_fusion.21
  28.7 1.5 constant_dynamic-update-slice_fusion.20
  30.2 1.5 constant_dynamic-update-slice_fusion.19
  33.1 1.5 constant_dynamic-update-slice_fusion.17
  34.6 1.5 constant_dynamic-update-slice_fusion.16
  36.1 1.5 constant_dynamic-update-slice_fusion.15
  37.5 1.5 constant_dynamic-update-slice_fusion.14
  39.0 1.5 constant_dynamic-update-slice_fusion.13
  40.5 1.5 constant_dynamic-update-slice_fusion.12
  41.9 1.5 constant_dynamic-update-slice_fusion.11
  43.4 1.5 constant_dynamic-update-slice_fusion.10
  44.8 1.5 constant_dynamic-update-slice_fusion.9
  47.8 1.5 constant_dynamic-update-slice_fusion.7
  49.2 1.5 constant_dynamic-update-slice_fusion.6
  53.6 1.5 constant_dynamic-update-slice_fusion.3
  59.2 4.9 %all-to-all-start = ((bf16[32,128,256]{2,1,0:T(8,128)(2,1)}), bf16[32,128,256]{2,1,0:T(8,128)(2,1)}, u32[]{:S(2)}, u32[]{:S(2)}) async-start(bf16[32,128,256]{2,1,0:T(8,128)(2,1)} %constant_dynamic-update-slice_fusion.1), calls=%async_computation | async-start | bytes 4194304 | tf_op jit(solution)/shard_map/all_to_all | solution.py:91
  64.1 72.7 %all-gather.1 = bf16[32,12,1024]{2,1,0:T(8,128)(2,1)S(1)} all-gather(bf16[1,12,1024]{2,1,0:T(8,128)(2,1)S(1)} %bitcast.166), channel_id=1, replica_groups=mesh['dp'=1,'ctx'=32] {'ctx'}, dimensions={0}, use_global_device_ids=true | all-gather | bytes 811008 | tf_op jit(solution)/shard_map/all_gather | solution.py:78
  138.5 41.9 %all-reduce = s32[384]{0:T(512)S(1)} all-reduce(s32[384]{0:T(512)S(1)} %dynamic-update-slice), channel_id=1, replica_groups=mesh['dp'=1,'ctx'=32] {'ctx'}, use_global_device_ids=true, to_apply=%add | all-reduce | flops 384 | bytes 3072
  180.5 37.8 %all-gather = s32[32,1,128]{2,1,0:T(1,128)S(1)} all-gather(s32[1,1,128]{2,1,0:T(1,128)S(1)} %bitcast.167), channel_id=1, replica_groups=mesh['dp'=1,'ctx'=32] {'ctx'}, dimensions={0}, use_global_device_ids=true | all-gather | bytes 16896 | tf_op jit(solution)/shard_map/all_gather | solution.py:98
  218.7 4.1 copy.69
  222.8 57.9 %while.27 = (s32[]{:T(128)}, f32[384,2,128]{0,2,1:T(8,128)S(1)}, f32[384,2,128]{0,2,1:T(8,128)}, bf16[4,1024,256]{2,1,0:T(8,128)(2,1)}, s32[4]{0:T(128)S(1)}, /*...) while((s32[]{:T(128)}, f32[384,2,128]{0,2,1:T(8,128)S(1)}, ...), condition=%wide.region_4.5_spmd.clone, body=%wide.region_0.4_spmd.clone.sunk | while | flops 1017117056 | bytes 52033364 | solution.py:59
  226.8 4.0 fusion.71
  230.8 2.7 fusion.73
  241.3 4.0 fusion.71
  245.3 2.7 fusion.73
  255.8 4.0 fusion.71
  259.7 2.7 fusion.73
  270.2 4.0 fusion.71
  274.2 2.7 fusion.73
  280.7 7.4 %all-to-all-start.2 = ((bf16[32,128,256]{2,1,0:T(8,128)(2,1)}), bf16[32,128,256]{2,1,0:T(8,128)(2,1)}, u32[]{:S(2)}, u32[]{:S(2)}) async-start(bf16[32,128,256]{2,1,0:T(8,128)(2,1)} %bitcast.159), calls=%async_computation.2 | async-start | bytes 4194304 | tf_op jit(solution)/shard_map/all_to_all | solution.py:102
  289.7 94.6 %fusion = bf16[16,1024]{1,0:T(8,128)(2,1)S(1)} fusion(bf16[384,1024]{1,0:T(8,128)(2,1)S(1)} %add_convert_fusion), kind=kCustom, calls=%all-reduce-scatter | all-reduce-scatter fusion | flops 524289 | bytes 819200
  385.8 8.5 %collective-permute-start.5 = (bf16[16,1024]{1,0:T(8,128)(2,1)S(1)}, bf16[16,1024]{1,0:T(8,128)(2,1)S(1)}, u32[]{:S(2)}, u32[]{:S(2)}) collective-permute-start(bf16[16,1024]{1,0:T(8,128)(2,1)S(1)} %fusion), channel_id=1, source_target_pairs={{0,6},{1,7},{2,8},{3,9},{4,10},{5,11},{6,12},{7,13},{8,14},{9,15},... | collective-permute-start | bytes 98312
  396.0 3.4 collective-permute-start.4
  399.5 1.9 collective-permute-start.3
  401.3 4.8 %collective-permute-start.2 = (bf16[16,1024]{1,0:T(8,128)(2,1)S(1)}, bf16[16,1024]{1,0:T(8,128)(2,1)}, u32[]{:S(2)}, u32[]{:S(2)}) collective-permute-start(bf16[16,1024]{1,0:T(8,128)(2,1)S(1)} %fusion), channel_id=1, source_target_pairs={{0,3},{1,4},{2,5},{3,6},{4,7},{5,8},{6,9},{7,10},{8,11},{9,12},{10... | collective-permute-start | bytes 98312
  406.1 2.5 collective-permute-start.1
  408.7 4.5 %collective-permute-start = (bf16[16,1024]{1,0:T(8,128)(2,1)S(1)}, bf16[16,1024]{1,0:T(8,128)(2,1)}, u32[]{:S(2)}, u32[]{:S(2)}) collective-permute-start(bf16[16,1024]{1,0:T(8,128)(2,1)S(1)} %fusion), channel_id=1, source_target_pairs={{0,1},{1,2},{2,3},{3,4},{4,5},{5,6},{6,7},{7,8},{8,9},{9,10},{10,1... | collective-permute-start | bytes 98312
  416.4 4.7 %concatenate = bf16[140,1024]{1,0:T(8,128)(2,1)S(1)} concatenate(bf16[12,1024]{1,0:T(8,128)(2,1)S(1)} %collective-permute-done.7, bf16[16,1024]{1,0:T(8,128)(2,1)S(1)} %collective-permute-done.6, bf16[16,1024]{1,0:T(8,128)(2,1)S(1)} %collective-permute-done.5, bf16[16,1024]{1,0:T(8,128)(2,1)} %collective-permute-done.4, bf16[16,1024]{1,0:T(8,128)(2,1)} %collective-permute-done.3, ...), dimensions={0} | concatenate | bytes 573440
  421.7 3.2 copy.73
  424.9 2.9 copy.74
  (144 shorter events, 56.0 us)
Async XLA Ops:
  0.6 217.6 %copy-start = (bf16[1024,256]{1,0:T(8,128)(2,1)S(1)}, bf16[1024,256]{1,0:T(8,128)(2,1)}, u32[]{:S(2)}) copy-start(bf16[1024,256]{1,0:T(8,128)(2,1)} %param.12) | copy-start | bytes 1572868
  4.8 54.4 %all-to-all-start.1 = ((bf16[128,32,256]{0,2,1:T(8,128)(2,1)}), bf16[128,32,256]{0,2,1:T(8,128)(2,1)S(1)}, u32[]{:S(2)}, u32[]{:S(2)}) async-start(bf16[128,32,256]{0,2,1:T(8,128)(2,1)} %bitcast.156), calls=%async_computation.1 | async-start | bytes 4194304 | tf_op jit(solution)/shard_map/all_to_all | solution.py:96
  58.0 6.1 %copy-start.11 = (bf16[12,1024]{1,0:T(8,128)(2,1)S(1)}, bf16[12,1024]{1,0:T(8,128)(2,1)}, u32[]{:S(2)}) copy-start(bf16[12,1024]{1,0:T(8,128)(2,1)} %param.11) | copy-start | bytes 73732
  59.2 4.9 %copy-start.2 = (bf16[128,32,256]{0,2,1:T(8,128)(2,1)}, bf16[128,32,256]{0,2,1:T(8,128)(2,1)S(1)}, u32[]{:S(2)}) copy-start(bf16[128,32,256]{0,2,1:T(8,128)(2,1)S(1)} %all-to-all-done.1) | copy-start | bytes 6291460
  59.2 163.6 %all-to-all-start = ((bf16[32,128,256]{2,1,0:T(8,128)(2,1)}), bf16[32,128,256]{2,1,0:T(8,128)(2,1)}, u32[]{:S(2)}, u32[]{:S(2)}) async-start(bf16[32,128,256]{2,1,0:T(8,128)(2,1)} %constant_dynamic-update-slice_fusion.1), calls=%async_computation | async-start | bytes 4194304 | tf_op jit(solution)/shard_map/all_to_all | solution.py:91
  64.1 72.9 %copy-start.3 = (bf16[1024,256]{1,0:T(8,128)(2,1)S(1)}, bf16[1024,256]{1,0:T(8,128)(2,1)}, u32[]{:S(2)}) copy-start(bf16[1024,256]{1,0:T(8,128)(2,1)} %param.13) | copy-start | bytes 1572868
  136.8 1.5 copy-start.13
  136.8 43.6 %copy-start.12 = (s32[128]{0:T(128)S(1)}, s32[128]{0:T(128)}, u32[]{:S(2)}) copy-start(s32[128]{0:T(128)} %param.14) | copy-start | bytes 1540
  226.8 4.0 copy-start.7
  230.8 2.8 copy-start.1
  230.8 2.8 copy-start.10
  233.6 0.7 copy-start.8
  241.3 4.0 copy-start.7
  245.2 2.8 copy-start.1
  245.3 2.8 copy-start.10
  248.1 0.7 copy-start.8
  255.8 4.0 copy-start.7
  259.7 2.8 copy-start.1
  259.7 2.8 copy-start.10
  262.6 0.7 copy-start.8
  270.2 4.0 copy-start.7
  274.2 2.8 copy-start.1
  274.2 2.8 copy-start.10
  277.0 0.7 copy-start.8
  280.7 7.5 %copy-start.9 = (f32[384,2,128]{0,2,1:T(8,128)S(1)}, f32[384,2,128]{0,2,1:T(8,128)}, u32[]{:S(2)}) copy-start(f32[384,2,128]{0,2,1:T(8,128)} %get-tuple-element.121) | copy-start | bytes 1179652
  280.7 141.0 %all-to-all-start.2 = ((bf16[32,128,256]{2,1,0:T(8,128)(2,1)}), bf16[32,128,256]{2,1,0:T(8,128)(2,1)}, u32[]{:S(2)}, u32[]{:S(2)}) async-start(bf16[32,128,256]{2,1,0:T(8,128)(2,1)} %bitcast.159), calls=%async_computation.2 | async-start | bytes 4194304 | tf_op jit(solution)/shard_map/all_to_all | solution.py:102
  288.2 1.1 copy-start.4
  288.2 0.7 copy-start.5
  384.3 28.9 %copy-start.6 = (bf16[384,2,128]{0,2,1:T(8,128)(2,1)S(1)}, bf16[384,2,128]{0,2,1:T(8,128)(2,1)}, u32[]{:S(2)}) copy-start(bf16[384,2,128]{0,2,1:T(8,128)(2,1)} %copy-done.5) | copy-start | bytes 589828
  384.4 21.8 %collective-permute-start.6 = (bf16[16,1024]{1,0:T(8,128)(2,1)S(1)}, bf16[16,1024]{1,0:T(8,128)(2,1)S(1)}, u32[]{:S(2)}, u32[]{:S(2)}) collective-permute-start(bf16[16,1024]{1,0:T(8,128)(2,1)S(1)} %fusion), channel_id=1, source_target_pairs={{0,7},{1,8},{2,9},{3,10},{4,11},{5,12},{6,13},{7,14},{8,15},{9,16}... | collective-permute-start | bytes 98312
  385.8 22.9 %collective-permute-start.5 = (bf16[16,1024]{1,0:T(8,128)(2,1)S(1)}, bf16[16,1024]{1,0:T(8,128)(2,1)S(1)}, u32[]{:S(2)}, u32[]{:S(2)}) collective-permute-start(bf16[16,1024]{1,0:T(8,128)(2,1)S(1)} %fusion), channel_id=1, source_target_pairs={{0,6},{1,7},{2,8},{3,9},{4,10},{5,11},{6,12},{7,13},{8,14},{9,15},... | collective-permute-start | bytes 98312
  394.3 7.1 %collective-permute-start.7 = (bf16[12,1024]{1,0:T(8,128)(2,1)S(1)}, bf16[12,1024]{1,0:T(8,128)(2,1)S(1)}, u32[]{:S(2)}, u32[]{:S(2)}) collective-permute-start(bf16[12,1024]{1,0:T(8,128)(2,1)S(1)} %slice), channel_id=1, source_target_pairs={{0,8},{1,9},{2,10},{3,11},{4,12},{5,13},{6,14},{7,15},{8,16},{9,17... | collective-permute-start | bytes 73736
  396.0 20.3 %collective-permute-start.4 = (bf16[16,1024]{1,0:T(8,128)(2,1)S(1)}, bf16[16,1024]{1,0:T(8,128)(2,1)}, u32[]{:S(2)}, u32[]{:S(2)}) collective-permute-start(bf16[16,1024]{1,0:T(8,128)(2,1)S(1)} %fusion), channel_id=1, source_target_pairs={{0,5},{1,6},{2,7},{3,8},{4,9},{5,10},{6,11},{7,12},{8,13},{9,14},{... | collective-permute-start | bytes 98312
  399.5 16.9 %collective-permute-start.3 = (bf16[16,1024]{1,0:T(8,128)(2,1)S(1)}, bf16[16,1024]{1,0:T(8,128)(2,1)}, u32[]{:S(2)}, u32[]{:S(2)}) collective-permute-start(bf16[16,1024]{1,0:T(8,128)(2,1)S(1)} %fusion), channel_id=1, source_target_pairs={{0,4},{1,5},{2,6},{3,7},{4,8},{5,9},{6,10},{7,11},{8,12},{9,13},{1... | collective-permute-start | bytes 98312
  401.3 15.0 %collective-permute-start.2 = (bf16[16,1024]{1,0:T(8,128)(2,1)S(1)}, bf16[16,1024]{1,0:T(8,128)(2,1)}, u32[]{:S(2)}, u32[]{:S(2)}) collective-permute-start(bf16[16,1024]{1,0:T(8,128)(2,1)S(1)} %fusion), channel_id=1, source_target_pairs={{0,3},{1,4},{2,5},{3,6},{4,7},{5,8},{6,9},{7,10},{8,11},{9,12},{10... | collective-permute-start | bytes 98312
  406.1 10.2 %collective-permute-start.1 = (bf16[16,1024]{1,0:T(8,128)(2,1)S(1)}, bf16[16,1024]{1,0:T(8,128)(2,1)}, u32[]{:S(2)}, u32[]{:S(2)}) collective-permute-start(bf16[16,1024]{1,0:T(8,128)(2,1)S(1)} %fusion), channel_id=1, source_target_pairs={{0,2},{1,3},{2,4},{3,5},{4,6},{5,7},{6,8},{7,9},{8,10},{9,11},{10,... | collective-permute-start | bytes 98312
  408.7 7.6 %collective-permute-start = (bf16[16,1024]{1,0:T(8,128)(2,1)S(1)}, bf16[16,1024]{1,0:T(8,128)(2,1)}, u32[]{:S(2)}, u32[]{:S(2)}) collective-permute-start(bf16[16,1024]{1,0:T(8,128)(2,1)S(1)} %fusion), channel_id=1, source_target_pairs={{0,1},{1,2},{2,3},{3,4},{4,5},{5,6},{6,7},{7,8},{8,9},{9,10},{10,1... | collective-permute-start | bytes 98312
